TPU v7x, 256 devices: a whole 4x4x8 slice. The times are simulated.
256 devices in a mesh: pipe: 16 (over x, z_lo, core), tensor: 16 (over y, z_hi).
Axes of the slice: x: 4, y: 4, z: 8 (z_hi: 4, z_lo: 2; z = z_hi * 2 + z_lo), core: 2. Of those that a mesh axis runs over, the one named last changes fastest.
Arguments:
- hidden: bfloat16 [384, 8192], P('pipe', 'tensor'), may hold values from -64 to 64
- weight: bfloat16 [8192, 131072], P(None, ('pipe', 'tensor')), may hold values from -0.23201941 to 0.23201941
- targets: int32 [384], replicated, may hold values from 0 to 131071
- token_weight: float32 [384], replicated, may hold values from 0.1 to 1
Outputs:
- token_loss: float32 [384], P('pipe')
- hidden_grad: float32 [384, 8192], P('pipe', 'tensor')
All inputs are finite; a program needn't handle non-finite values.
Results may differ from a plain program's by a relative error of at most 0.0029.
Values may be sent and summed in bfloat16 or wider, within the bound.
No kernel may reach another device: no remote copies, remote signals or barrier semaphores. Data moves between devices by JAX's collectives and lax.ppermute only.
A program may use at most 128 MiB of HBM per device.

v0:
```python
import jax
import jax.numpy as jnp
from jax import lax
from jax.sharding import Mesh
from jax.sharding import PartitionSpec as P

TENSOR = ("tensor_0", "tensor_1")
PIPE = ("pipe_0", "pipe_1", "pipe_2")
PIPE_TENSOR = ("pipe_0", "pipe_1", "pipe_2", "tensor_0", "tensor_1")
loss_scale = 32.0


def sent_to_all(shard, axis):
    copies = jnp.broadcast_to(shard, (lax.axis_size(axis), *shard.shape))
    return lax.all_to_all(copies, axis, split_axis=0, concat_axis=0, tiled=True)


def joined_along(blocks, dim):
    blocks = jnp.moveaxis(blocks, 0, dim)
    lengths = blocks.shape
    return blocks.reshape(*lengths[:dim], lengths[dim] * lengths[dim + 1], *lengths[dim + 2 :])


def gather_directly(shard, axis, dim):
    blocks = sent_to_all(shard, axis)
    return joined_along(blocks, dim)


def all_in_one(shard, axis):
    leaves = jax.tree.leaves(shard)
    order = sorted(range(len(leaves)), key=lambda k: -leaves[k].size)
    width = (1, *leaves[order[0]].shape)[-1]
    lines = [
        jnp.pad(leaves[k].reshape(-1), (0, -leaves[k].size % width)).reshape(-1, width)
        for k in order
    ]
    both, at, found = (lax.all_gather(jnp.concatenate(lines), axis), 0, {})
    for k, line in zip(order, lines):
        piece = both[:, at : at + len(line)].reshape(len(both), -1)
        found[k] = piece[:, : leaves[k].size].reshape(-1, *leaves[k].shape)
        at += len(line)
    numbers = iter(range(len(leaves)))
    return jax.tree.map(lambda _: found[next(numbers)], shard)


def joined_all(shard, axes, combine):
    for axis in axes:
        pieces = all_in_one(shard, axis)
        shard = jax.tree.map(lambda part: part[0], pieces)
        for k in range(1, lax.axis_size(axis)):
            shard = combine(shard, jax.tree.map(lambda part: part[k], pieces))
    return shard


def cut_along(shard, dim, count):
    lengths = shard.shape
    blocks = shard.reshape(*lengths[:dim], count, lengths[dim] // count, *lengths[dim + 1 :])
    return jnp.moveaxis(blocks, dim, 0)


def sent_and_summed(shard, axis, dim):
    count = lax.axis_size(axis)
    blocks = lax.all_to_all(cut_along(shard, dim, count), axis, 0, 0, tiled=True)
    return jnp.sum(blocks, axis=0)


def combine_stats(left_stats, right_stats):
    left_peak, left_total, left_target = left_stats
    right_peak, right_total, right_target = right_stats
    joined = jnp.maximum(left_peak, right_peak)
    summed = left_total * jnp.exp(left_peak - joined) + right_total * jnp.exp(right_peak - joined)
    return (joined, summed, left_target + right_target)


def local(hidden, weight, targets, token_weight):
    rows_local = hidden.shape[0]
    width_local = weight.shape[1]
    full_rows = gather_directly(hidden, TENSOR, 1)
    logits = jnp.dot(
        lax.all_gather(full_rows, PIPE, axis=0, tiled=True),
        weight,
        preferred_element_type=jnp.float32,
    )
    device_block = lax.axis_index(PIPE) * lax.axis_size(TENSOR) + lax.axis_index(TENSOR)
    columns = device_block * width_local + jnp.arange(width_local, dtype=jnp.int32)
    target_hit = targets[:, None] == columns[None, :]
    chosen = jnp.sum(jnp.where(target_hit, logits, jnp.float32(0.0)), axis=1)
    local_peak = jnp.max(logits, axis=1)
    local_total = jnp.sum(jnp.exp(logits - local_peak[:, None]), axis=1)
    global_peak, global_total, target_logit = joined_all(
        (local_peak, local_total, chosen), PIPE_TENSOR, combine_stats
    )
    log_total = global_peak + jnp.log(global_total)
    loss_rows = log_total - target_logit
    token_loss = lax.dynamic_slice_in_dim(
        loss_rows, lax.axis_index(PIPE) * rows_local, rows_local, 0
    )
    softmax = jnp.exp(logits - log_total[:, None])
    dlogits = (
        loss_scale * token_weight[:, None] * (softmax - target_hit.astype(jnp.float32))
    ).astype(jnp.bfloat16)
    section_part = lax.psum_scatter(
        lax.dot_general(
            dlogits, weight, (((1,), (1,)), ((), ())), preferred_element_type=jnp.float32
        ),
        PIPE,
        scatter_dimension=0,
        tiled=True,
    )
    hidden_grad = sent_and_summed(section_part, TENSOR, 1)
    return (token_loss, hidden_grad)


def solution(mesh):
    split = Mesh(
        mesh.devices.reshape(4, 2, 2, 4, 4), ("pipe_0", "pipe_1", "pipe_2", "tensor_0", "tensor_1")
    )
    placed = (P(PIPE, TENSOR), P(None, PIPE_TENSOR), P(), P())
    return jax.shard_map(
        local, mesh=split, in_specs=placed, out_specs=(P(PIPE), P(PIPE, TENSOR)), check_vma=False
    )
```

profile of v0, /device:TPU:4, one launch (start us, length us, event | category | flops | bytes accessed | tf_op | source)
XLA Modules:
  0.0 324.7 jit_solution(18209849761081258595)
XLA Ops:
  7.2 0.0 all-gather.12.cloned.1.call-start
  7.2 0.8 broadcast_in_dim.6
  8.0 27.0 %all_to_all.10 = bf16[16,24,512]{2,1,0:T(8,128)(2,1)S(1)} all-to-all(bf16[16,24,512]{2,1,0:T(8,128)(2,1)S(1)} %broadcast_in_dim.6), channel_id=1, replica_groups=mesh['pipe_0'=4,'pipe_1'=2,'pipe_2'=2,'tensor_0'=4,'tensor_1'=4] {'tenso..., dimensions={0} | all-to-all | bytes 786432 | tf_op jit(solution)/shard_map/all_to_all | solution.py:15
  35.0 0.8 copy.9
  35.8 0.0 all-gather.12.cloned.1.call-update
  35.8 0.0 reduce-scatter.2.cloned.1.call-start
  35.9 0.7 broadcast_multiply_fusion
  36.6 38.5 %all-gather.12.cloned.1.call-done = bf16[384,8192]{1,0:T(8,128)(2,1)} async-done(((bf16[24,8192]{1,0:T(8,128)(2,1)}), bf16[384,8192]{1,0:T(8,128)(2,1)}) %all-gather.12.cloned.1.call-update) | async-done | bytes 6291472 | tf_op jit(solution)/shard_map/all_gather | solution.py:80
  75.1 8.0 %fusion.58 = (f32[384]{0:T(512)S(1)}, f32[384,512]{1,0:T(8,128)S(1)}) fusion(bf16[384,8192]{1,0:T(8,128)(2,1)} %all-gather.12.cloned.1.call-done, bf16[8192,512]{1,0:T(8,128)(2,1)} %param.5), kind=kOutput, calls=%fused_computation.111 | convolution fusion | flops 3221421568 | bytes 15468032 | tf_op jit(solution)/shard_map/dot_general | solution.py:79
  83.1 0.4 exponential_reduce_fusion
  83.5 11.0 %all-gather.5 = f32[4,3,384]{2,1,0:T(4,128)S(1)} all-gather(f32[1,3,384]{2,1,0:T(4,128)S(1)} %maximum_bitcast_fusion), channel_id=2, replica_groups=mesh['pipe_0'=4,'pipe_1'=2,'pipe_2'=2,'tensor_0'=4,'tensor_1'=4] {'pipe_0'}, dimensions={0}, use_global_device_ids=true | all-gather | bytes 23040 | tf_op jit(solution)/shard_map/all_gather | solution.py:37
  94.6 4.4 %all-gather.6 = f32[2,3,384]{2,1,0:T(4,128)S(1)} all-gather(f32[1,3,384]{2,1,0:T(4,128)S(1)} %maximum_bitcast_fusion.1), channel_id=3, replica_groups=mesh['pipe_0'=4,'pipe_1'=2,'pipe_2'=2,'tensor_0'=4,'tensor_1'=4] {'pipe_1'}, dimensions={0}, use_global_device_ids=true | all-gather | bytes 13824 | tf_op jit(solution)/shard_map/all_gather | solution.py:37
  99.1 1.8 all-gather.7
  100.9 12.3 %all-gather.8 = f32[4,3,384]{2,1,0:T(4,128)S(1)} all-gather(f32[1,3,384]{2,1,0:T(4,128)S(1)} %maximum_bitcast_fusion.3), channel_id=5, replica_groups=mesh['pipe_0'=4,'pipe_1'=2,'pipe_2'=2,'tensor_0'=4,'tensor_1'=4] {'tenso..., dimensions={0}, use_global_device_ids=true | all-gather | bytes 23040 | tf_op jit(solution)/shard_map/all_gather | solution.py:37
  113.3 15.7 %all-gather.9 = f32[4,3,384]{2,1,0:T(4,128)S(1)} all-gather(f32[1,3,384]{2,1,0:T(4,128)S(1)} %maximum_bitcast_fusion.4), channel_id=6, replica_groups=mesh['pipe_0'=4,'pipe_1'=2,'pipe_2'=2,'tensor_0'=4,'tensor_1'=4] {'tenso..., dimensions={0}, use_global_device_ids=true | all-gather | bytes 23040 | tf_op jit(solution)/shard_map/all_gather | solution.py:37
  129.0 0.1 fusion.16
  129.0 12.0 %fusion.4 = f32[384,8192]{1,0:T(8,128)} fusion(bf16[8192,512]{1,0:T(8,128)(2,1)} %param.5, f32[384,512]{1,0:T(8,128)S(1)} %get-tuple-element.24, f32[384]{0:T(512)S(1)} %get-tuple-element.14, f32[384]{0:T(512)S(1)} %broadcast_multiply_fusion, s32[512]{0:T(512)S(1)} %iota_add_fusion, s32[384]{0:T(512)S(1)} %copy-done), kind=kOutput, calls=%fused_computation.8 | convolution fusion | flops 3222405120 | bytes 21764608 | tf_op jit(solution)/shard_map/dot_general | solution.py:103
  141.1 0.0 reduce-scatter.2.cloned.1.call-update
  141.1 139.7 %reduce-scatter.2.cloned.1.call-done = f32[24,8192]{1,0:T(8,128)} async-done(((f32[384,8192]{1,0:T(8,128)}), f32[24,8192]{1,0:T(8,128)}) %reduce-scatter.2.cloned.1.call-update) | async-done | bytes 786448 | tf_op jit(solution)/shard_map/reduce_scatter | solution.py:102
  280.8 2.1 copy.11
  282.9 8.7 %all-to-all-start.1 = ((f32[16,24,512]{2,1,0:T(8,128)}), f32[16,24,512]{2,1,0:T(8,128)S(1)}, u32[]{:S(2)}, u32[]{:S(2)}) async-start(f32[16,24,512]{2,1,0:T(8,128)} %bitcast.226), calls=%async_computation.2 | async-start | bytes 1572864 | tf_op jit(solution)/shard_map/all_to_all | solution.py:63
  291.6 0.6 dynamic_slice.3
  292.2 25.0 %all-to-all-done.1 = f32[16,24,512]{2,1,0:T(8,128)S(1)} async-done(((f32[16,24,512]{2,1,0:T(8,128)}), f32[16,24,512]{2,1,0:T(8,128)S(1)}, u32[]{:S(2)}, u32[]{:S(2)}) %all-to-all-start.1) | async-done | bytes 786464 | tf_op jit(solution)/shard_map/all_to_all | solution.py:63
  317.2 0.7 reduce_sum.29
  (20 shorter events, 0.2 us)
Async XLA Ops:
  7.2 67.9 %all-gather.12.cloned.1.call-start = ((), (), s32[]{:S(2)}) async-start(), calls=%async_computation.3 | async-start | bytes 6684672 | tf_op jit(solution)/shard_map/all_gather | solution.py:80
  35.8 245.0 %reduce-scatter.2.cloned.1.call-start = ((), (), s32[]{:S(2)}) async-start(), calls=%async_computation.4 | async-start | bytes 13369344 | tf_op jit(solution)/shard_map/reduce_scatter | solution.py:102
  36.6 46.6 %copy-start = (s32[384]{0:T(512)S(1)}, s32[384]{0:T(512)}, u32[]{:S(2)}) copy-start(s32[384]{0:T(512)} %param.6) | copy-start | bytes 4612
  282.9 34.3 %all-to-all-start.1 = ((f32[16,24,512]{2,1,0:T(8,128)}), f32[16,24,512]{2,1,0:T(8,128)S(1)}, u32[]{:S(2)}, u32[]{:S(2)}) async-start(f32[16,24,512]{2,1,0:T(8,128)} %bitcast.226), calls=%async_computation.2 | async-start | bytes 1572864 | tf_op jit(solution)/shard_map/all_to_all | solution.py:63
Sparse Core Ops, SparseCore 0:
  35.9 39.1 all-gather.11
  141.2 139.5 reduce-scatter.1
where the time goes:
time: 325 us
  waiting for transfers between devices  203 us (62%)
  blocking collectives  72.2 us (22%)
  matrix products  20 us (6%)
  between operations  14.2 us (4%)
  starting transfers between devices  8.76 us (3%)
  local copies, waits for them, and re-layouts  4.22 us (1%)
    reduce_scatter x1, waiting for transfers between devices, local(): lax.psum_scatter(lax.dot_general(dlogits, weight, (((1,), (1,)), ((), ())...  140 us
    all_gather x5, blocking collectives, all_in_one(): both, at, found = (lax.all_gather(jnp.concatenate(lines), axis), 0, {})  45.2 us
    all_gather x1, waiting for transfers between devices, local(): lax.all_gather(full_rows, PIPE, axis=0, tiled=True)  38.5 us
    all_to_all x1, blocking collectives, sent_to_all(): return lax.all_to_all(copies, axis, split_axis=0, concat_axis=0, tiled=True)  27 us
    all_to_all x1, waiting for transfers between devices, sent_and_summed(): lax.all_to_all(cut_along(shard, dim, count), axis, 0, 0, tiled=True)  25 us
    dot_general x1, matrix products, local(): lax.dot_general(dlogits, weight, (((1,), (1,)), ((), ())), preferred_elem...  12 us
    all_to_all x1, starting transfers between devices, sent_and_summed(): lax.all_to_all(cut_along(shard, dim, count), axis, 0, 0, tiled=True)  8.68 us
    dot_general x1, matrix products, local(): jnp.dot(lax.all_gather(full_rows, PIPE, axis=0, tiled=True), weight, pref...  8 us
  transfers between devices with their start and end apart: 3, of which 3 were waited for; matrix products, arithmetic and copies ran while one was open for 0% of the time, Pallas kernels for 0%

commit v1 on v0

--- a/solution.py
+++ b/solution.py
@@ -76,11 +76,13 @@
     rows_local = hidden.shape[0]
     width_local = weight.shape[1]
     full_rows = gather_directly(hidden, TENSOR, 1)
-    logits = jnp.dot(
-        lax.all_gather(full_rows, PIPE, axis=0, tiled=True),
-        weight,
-        preferred_element_type=jnp.float32,
-    )
+
+    def outputs_launch(d_out, mat):
+        y2 = jnp.stack([mat for _ in range(lax.axis_size(PIPE))], axis=0)
+        later = lax.all_to_all(y2, PIPE, 0, 0)
+        return jnp.concatenate(later, d_out)
+
+    logits = jnp.dot(outputs_launch(0, full_rows), weight, preferred_element_type=jnp.float32)
     device_block = lax.axis_index(PIPE) * lax.axis_size(TENSOR) + lax.axis_index(TENSOR)
     columns = device_block * width_local + jnp.arange(width_local, dtype=jnp.int32)
     target_hit = targets[:, None] == columns[None, :]

time: 325 us -> 361 us (1.11)
  waiting for transfers between devices: 203 us -> 232 us
  starting transfers between devices: 8.76 us -> 14.1 us
    all_to_all x0 -> x1, waiting for transfers between devices: none -> 70.2 us  [outputs_launch(): later = lax.all_to_all(y2, PIPE, 0, 0)]
    all_gather x1 -> x0, waiting for transfers between devices: 38.5 us -> none  [local(): lax.all_gather(full_rows, PIPE, axis=0, tiled=True)]
    all_to_all x0 -> x1, starting transfers between devices: none -> 5.44 us  [outputs_launch(): later = lax.all_to_all(y2, PIPE, 0, 0)]
where the time goes in v1:
time: 361 us; the launch traced here: 360 us
  waiting for transfers between devices  232 us (64%)
  blocking collectives  71.5 us (20%)
  matrix products  20 us (6%)
  between operations  14.2 us (4%)
  starting transfers between devices  14.1 us (4%)
  local copies, waits for them, and re-layouts  6.85 us (2%)
    reduce_scatter x1, waiting for transfers between devices, local(): lax.psum_scatter(lax.dot_general(dlogits, weight, (((1,), (1,)), ((), ())...  137 us
    all_to_all x1, waiting for transfers between devices, outputs_launch(): later = lax.all_to_all(y2, PIPE, 0, 0)  70.2 us
    all_gather x5, blocking collectives, all_in_one(): both, at, found = (lax.all_gather(jnp.concatenate(lines), axis), 0, {})  44.5 us
    all_to_all x1, blocking collectives, sent_to_all(): return lax.all_to_all(copies, axis, split_axis=0, concat_axis=0, tiled=True)  27 us
    all_to_all x1, waiting for transfers between devices, sent_and_summed(): lax.all_to_all(cut_along(shard, dim, count), axis, 0, 0, tiled=True)  25 us
    dot_general x1, matrix products, local(): lax.dot_general(dlogits, weight, (((1,), (1,)), ((), ())), preferred_elem...  12 us
    all_to_all x1, starting transfers between devices, sent_and_summed(): lax.all_to_all(cut_along(shard, dim, count), axis, 0, 0, tiled=True)  8.66 us
    dot_general x1, matrix products, local(): jnp.dot(outputs_launch(0, full_rows), weight, preferred_element_type=jnp....  8.02 us
  transfers between devices with their start and end apart: 3, of which 3 were waited for; matrix products, arithmetic and copies ran while one was open for 0% of the time, Pallas kernels for 0%

profile of v1, /device:TPU:4, one launch (start us, length us, event | category | flops | bytes accessed | tf_op | source)
XLA Modules:
  0.0 360.4 jit_solution(11353937692345249856)
XLA Ops:
  7.2 0.8 broadcast_in_dim.6
  7.9 27.0 %all_to_all.15 = bf16[16,24,512]{2,1,0:T(8,128)(2,1)S(1)} all-to-all(bf16[16,24,512]{2,1,0:T(8,128)(2,1)S(1)} %broadcast_in_dim.6), channel_id=1, replica_groups=mesh['pipe_0'=4,'pipe_1'=2,'pipe_2'=2,'tensor_0'=4,'tensor_1'=4] {'tenso..., dimensions={0} | all-to-all | bytes 786432 | tf_op jit(solution)/shard_map/all_to_all | solution.py:15
  35.0 3.4 stack.3
  38.4 5.4 %all-to-all-start.1 = ((bf16[16,24,8192]{2,1,0:T(8,128)(2,1)}), bf16[16,24,8192]{2,1,0:T(8,128)(2,1)}, u32[]{:S(2)}, u32[]{:S(2)}) async-start(bf16[16,24,8192]{2,1,0:T(8,128)(2,1)} %stack.3), calls=%async_computation.1 | async-start | bytes 12582912 | tf_op jit(solution)/shard_map/all_to_all | solution.py:82
  43.8 0.0 reduce-scatter.2.cloned.1.call-start
  43.9 70.2 %all-to-all-done.1 = bf16[16,24,8192]{2,1,0:T(8,128)(2,1)} async-done(((bf16[16,24,8192]{2,1,0:T(8,128)(2,1)}), bf16[16,24,8192]{2,1,0:T(8,128)(2,1)}, u32[]{:S(2)}, u32[]{:S(2)}) %all-to-all-start.1) | async-done | bytes 6291488 | tf_op jit(solution)/shard_map/all_to_all | solution.py:82
  114.1 8.0 %fusion.58 = (f32[384]{0:T(512)S(1)}, f32[384,512]{1,0:T(8,128)S(1)}) fusion(bf16[384,8192]{1,0:T(8,128)(2,1)} %bitcast.1, bf16[8192,512]{1,0:T(8,128)(2,1)} %param.5), kind=kOutput, calls=%fused_computation.111 | convolution fusion | flops 3221421568 | bytes 15468032 | tf_op jit(solution)/shard_map/dot_general | solution.py:85
  122.1 0.0 copy-done
  122.1 0.4 exponential_reduce_fusion
  122.5 12.6 %all-gather.5 = f32[4,3,384]{2,1,0:T(4,128)S(1)} all-gather(f32[1,3,384]{2,1,0:T(4,128)S(1)} %maximum_bitcast_fusion), channel_id=2, replica_groups=mesh['pipe_0'=4,'pipe_1'=2,'pipe_2'=2,'tensor_0'=4,'tensor_1'=4] {'pipe_0'}, dimensions={0}, use_global_device_ids=true | all-gather | bytes 23040 | tf_op jit(solution)/shard_map/all_gather | solution.py:37
  135.2 4.4 %all-gather.6 = f32[2,3,384]{2,1,0:T(4,128)S(1)} all-gather(f32[1,3,384]{2,1,0:T(4,128)S(1)} %maximum_bitcast_fusion.1), channel_id=3, replica_groups=mesh['pipe_0'=4,'pipe_1'=2,'pipe_2'=2,'tensor_0'=4,'tensor_1'=4] {'pipe_1'}, dimensions={0}, use_global_device_ids=true | all-gather | bytes 13824 | tf_op jit(solution)/shard_map/all_gather | solution.py:37
  139.6 1.8 all-gather.7
  141.5 12.0 %all-gather.8 = f32[4,3,384]{2,1,0:T(4,128)S(1)} all-gather(f32[1,3,384]{2,1,0:T(4,128)S(1)} %maximum_bitcast_fusion.3), channel_id=5, replica_groups=mesh['pipe_0'=4,'pipe_1'=2,'pipe_2'=2,'tensor_0'=4,'tensor_1'=4] {'tenso..., dimensions={0}, use_global_device_ids=true | all-gather | bytes 23040 | tf_op jit(solution)/shard_map/all_gather | solution.py:37
  153.5 13.8 %all-gather.9 = f32[4,3,384]{2,1,0:T(4,128)S(1)} all-gather(f32[1,3,384]{2,1,0:T(4,128)S(1)} %maximum_bitcast_fusion.4), channel_id=6, replica_groups=mesh['pipe_0'=4,'pipe_1'=2,'pipe_2'=2,'tensor_0'=4,'tensor_1'=4] {'tenso..., dimensions={0}, use_global_device_ids=true | all-gather | bytes 23040 | tf_op jit(solution)/shard_map/all_gather | solution.py:37
  167.3 0.1 fusion.16
  167.3 0.0 copy-done.1
  167.4 12.0 %fusion.4 = f32[384,8192]{1,0:T(8,128)} fusion(bf16[8192,512]{1,0:T(8,128)(2,1)} %param.5, f32[384,512]{1,0:T(8,128)S(1)} %get-tuple-element.24, f32[384]{0:T(512)S(1)} %get-tuple-element.14, f32[384]{0:T(512)S(1)} %get-tuple-element.25, s32[512]{0:T(512)S(1)} %iota_add_fusion, s32[384]{0:T(512)S(1)} %copy-done), kind=kOutput, calls=%fused_computation.8 | convolution fusion | flops 3222405120 | bytes 21764608 | tf_op jit(solution)/shard_map/dot_general | solution.py:105
  179.4 0.0 reduce-scatter.2.cloned.1.call-update
  179.4 137.1 %reduce-scatter.2.cloned.1.call-done = f32[24,8192]{1,0:T(8,128)} async-done(((f32[384,8192]{1,0:T(8,128)}), f32[24,8192]{1,0:T(8,128)}) %reduce-scatter.2.cloned.1.call-update) | async-done | bytes 786448 | tf_op jit(solution)/shard_map/reduce_scatter | solution.py:104
  316.5 2.1 copy.11
  318.5 8.7 %all-to-all-start.2 = ((f32[16,24,512]{2,1,0:T(8,128)}), f32[16,24,512]{2,1,0:T(8,128)S(1)}, u32[]{:S(2)}, u32[]{:S(2)}) async-start(f32[16,24,512]{2,1,0:T(8,128)} %bitcast.227), calls=%async_computation.3 | async-start | bytes 1572864 | tf_op jit(solution)/shard_map/all_to_all | solution.py:63
  327.2 0.6 dynamic_slice.3
  327.8 25.0 %all-to-all-done.2 = f32[16,24,512]{2,1,0:T(8,128)S(1)} async-done(((f32[16,24,512]{2,1,0:T(8,128)}), f32[16,24,512]{2,1,0:T(8,128)S(1)}, u32[]{:S(2)}, u32[]{:S(2)}) %all-to-all-start.2) | async-done | bytes 786464 | tf_op jit(solution)/shard_map/all_to_all | solution.py:63
  352.8 0.7 reduce_sum.29
  (21 shorter events, 0.2 us)
Async XLA Ops:
  38.4 75.7 %all-to-all-start.1 = ((bf16[16,24,8192]{2,1,0:T(8,128)(2,1)}), bf16[16,24,8192]{2,1,0:T(8,128)(2,1)}, u32[]{:S(2)}, u32[]{:S(2)}) async-start(bf16[16,24,8192]{2,1,0:T(8,128)(2,1)} %stack.3), calls=%async_computation.1 | async-start | bytes 12582912 | tf_op jit(solution)/shard_map/all_to_all | solution.py:82
  43.8 272.7 %reduce-scatter.2.cloned.1.call-start = ((), (), s32[]{:S(2)}) async-start(), calls=%async_computation.4 | async-start | bytes 13369344 | tf_op jit(solution)/shard_map/reduce_scatter | solution.py:104
  114.1 8.0 %copy-start = (s32[384]{0:T(512)S(1)}, s32[384]{0:T(512)}, u32[]{:S(2)}) copy-start(s32[384]{0:T(512)} %param.6) | copy-start | bytes 4612
  114.1 53.2 %copy-start.1 = (f32[384]{0:T(512)S(1)}, f32[384]{0:T(512)}, u32[]{:S(2)}) copy-start(f32[384]{0:T(512)} %param.7) | copy-start | bytes 4612
  318.5 34.3 %all-to-all-start.2 = ((f32[16,24,512]{2,1,0:T(8,128)}), f32[16,24,512]{2,1,0:T(8,128)S(1)}, u32[]{:S(2)}, u32[]{:S(2)}) async-start(f32[16,24,512]{2,1,0:T(8,128)} %bitcast.227), calls=%async_computation.3 | async-start | bytes 1572864 | tf_op jit(solution)/shard_map/all_to_all | solution.py:63
Sparse Core Ops, SparseCore 0:
  179.5 136.9 reduce-scatter.1
